TPU v7x, 32 devices: a whole 2x2x4 slice. The times are simulated.
32 devices in a mesh: seq: 4 (over y, x), res: 8 (over z, core).
Axes of the slice: x: 2, y: 2, z: 4, core: 2. Of those that a mesh axis runs over, the one named last changes fastest.
Arguments:
- alignment: float32 [256, 64, 256], P('seq', 'res'), may hold values from -100 to 100
- pair_features: float32 [64, 64, 128], P('seq', 'res'), may hold values from -100 to 100
- outer_gain: float32 [256], replicated, may hold values from 0.5 to 1.5
- w_outer_in: float32 [256, 64], replicated, may hold values from -0.375 to 0.375
- w_outer_out: float32 [1024, 128], replicated, may hold values from -0.1875 to 0.1875
- pair_gain: float32 [128], replicated, may hold values from 0.5 to 1.5
- w_bias: float32 [128, 8], replicated, may hold values from -30 to 30
- row_gain: float32 [256], replicated, may hold values from 0.5 to 1.5
- w_project: float32 [256, 1024], replicated, may hold values from -0.375 to 0.375
- w_output: float32 [256, 256], replicated, may hold values from -0.375 to 0.375
Outputs:
- alignment_out: float32 [256, 64, 256], P('seq', 'res')
- updated_pair_array: float32 [64, 64, 128], P('seq', 'res')
All inputs are finite; a program needn't handle non-finite values.
Results may differ from a plain program's by a relative error of at most 0.00018.
Values sent between devices are 32-bit elements; how exact they have to be, the bound alone decides.
A program may use at most 128 MiB of HBM per device.

v0:
```python
import jax
import jax.numpy as jnp
from jax import lax
from jax.sharding import PartitionSpec as P

precise = lax.Precision.HIGHEST


def layer_norm(values, scales):
    average = jnp.mean(values, axis=-1, keepdims=True)
    centered = values - average
    variance = jnp.mean(centered * centered, axis=-1, keepdims=True)
    return centered * lax.rsqrt(variance + 1e-05) * scales


def row_attention(sequence, bias_all, row_gain, w_project, w_output):
    residues, channels = sequence.shape
    head_count = bias_all.shape[0]
    head_size = channels // head_count
    normed_rows = layer_norm(sequence, row_gain)
    projected = jnp.dot(
        normed_rows, w_project, precision=precise, preferred_element_type=jnp.float32
    )
    query_map = projected[:, :channels].reshape(residues, head_count, head_size) * head_size ** (
        -0.5
    )
    key_map = projected[:, channels : 2 * channels].reshape(residues, head_count, head_size)
    value_map = projected[:, 2 * channels : 3 * channels].reshape(residues, head_count, head_size)
    gate_map = projected[:, 3 * channels :]
    scores = jnp.einsum("ihd,jhd->hij", query_map, key_map, precision=precise) + bias_all
    weights = jax.nn.softmax(scores, axis=-1)
    mixed_heads = jnp.einsum("hij,jhd->ihd", weights, value_map, precision=precise).reshape(
        residues, channels
    )
    gated_out = jax.nn.sigmoid(gate_map) * mixed_heads
    return sequence + jnp.dot(
        gated_out, w_output, precision=precise, preferred_element_type=jnp.float32
    )


def on_device(
    alignment,
    pair_features,
    outer_gain,
    w_outer_in,
    w_outer_out,
    pair_gain,
    w_bias,
    row_gain,
    w_project,
    w_output,
):
    sequence_local_count, residue_local_count, alignment_channel_count = alignment.shape
    row_block = pair_features.shape[0]
    sequence_group_list = lax.axis_size("res")
    seq_groups = lax.axis_size("seq")
    seq_total = sequence_local_count * seq_groups
    channels = w_outer_in.shape[1] // 2
    normed_rows = layer_norm(alignment, outer_gain)
    both_maps = jnp.einsum("src,cd->sdr", normed_rows, w_outer_in, precision=precise)
    left_maps = both_maps[:, :channels]
    right_maps = both_maps[:, channels:]
    left_all = lax.all_gather(left_maps, "res", axis=2, tiled=True)
    left_rows = lax.all_to_all(left_all, "seq", split_axis=2, concat_axis=0, tiled=True)
    product = jnp.einsum(
        "sxi,syj->ijxy",
        left_rows,
        lax.all_gather(right_maps, "seq", axis=0, tiled=True),
        precision=precise,
    )
    summed = product.reshape(row_block, residue_local_count, channels * channels)
    pair_update = jnp.einsum("ijk,kc->ijc", summed / seq_total, w_outer_out, precision=precise)
    updated_pair_array = pair_features + pair_update
    bias_tile = jnp.einsum(
        "ijc,ch->hij", layer_norm(updated_pair_array, pair_gain), w_bias, precision=precise
    )
    bias_rows = lax.all_gather(bias_tile, "res", axis=2, tiled=True)
    bias_all = lax.all_gather(bias_rows, "seq", axis=1, tiled=True)
    sequence_grouped_rows = alignment.reshape(
        sequence_group_list,
        sequence_local_count // sequence_group_list,
        residue_local_count,
        alignment_channel_count,
    )
    sequences = lax.all_to_all(
        sequence_grouped_rows, "res", split_axis=0, concat_axis=2, tiled=True
    )[0]
    updated = jax.vmap(row_attention, in_axes=(0, None, None, None, None))(
        sequences, bias_all, row_gain, w_project, w_output
    )
    attended = updated[None]
    returned_result = lax.all_to_all(attended, "res", split_axis=2, concat_axis=0, tiled=True)
    return (
        returned_result.reshape(sequence_local_count, residue_local_count, alignment_channel_count),
        updated_pair_array,
    )


def solution(mesh):
    in_specs = (
        P("seq", "res", None),
        P("seq", "res", None),
        P(),
        P(),
        P(),
        P(),
        P(),
        P(),
        P(),
        P(),
    )
    out_specs = (P("seq", "res", None), P("seq", "res", None))
    return jax.shard_map(
        on_device, mesh=mesh, in_specs=in_specs, out_specs=out_specs, check_vma=False
    )
```

profile of v0, /device:TPU:0, one launch (start us, length us, event | category | flops | bytes accessed | tf_op | source)
XLA Modules:
  0.0 148.9 jit_solution(3641051938862273192)
XLA Ops:
  0.6 0.0 copy-start
  0.6 1.3 reduce_sum.65
  1.9 1.3 multiply_reduce_fusion
  3.2 1.7 %convolution_bitcast_fusion = f32[64,64,8]{1,2,0:T(8,128)S(1)} fusion(f32[64,8,256]{2,1,0:T(8,128)} %param.10, f32[256]{0:T(256)} %param.12, f32[64,8]{1,0:T(8,128)S(1)} %add_rsqrt_fusion, f32[64,8]{1,0:T(8,128)S(1)} %broadcast_multiply_fusion, f32[256,64]{0,1:T(8,128)} %param.13), kind=kOutput, calls=%fused_computation.8 | convolution fusion | flops 101056512 | bytes 726016 | tf_op jit(solution)/shard_map/src,cd->sdr/dot_general | solution.py:60
  4.9 0.1 fusion.40
  5.1 25.1 %all_gather.13 = f32[64,32,64]{1,2,0:T(8,128)S(1)} all-gather(f32[64,32,8]{1,2,0:T(8,128)S(1)} %get-tuple-element.5), channel_id=1, replica_groups=mesh['seq'=4,'res'=8] {'res'}, dimensions={2}, use_global_device_ids=true | all-gather | bytes 589824 | tf_op jit(solution)/shard_map/all_gather | solution.py:63
  30.2 2.1 %copy.39 = f32[64,32,64]{0,1,2:T(8,128)} copy(f32[64,32,64]{1,2,0:T(8,128)S(1)} %all_gather.13) | data formatting | bytes 1048576 | tf_op jit(solution)/shard_map/all_gather | solution.py:63
  32.3 2.7 %reshape.99 = f32[4,1,32768]{2,1,0:T(1,128)} reshape(f32[64,32,64]{2,1,0:T(8,128)} %bitcast.73) | data formatting | bytes 1048576
  35.0 3.7 %all-to-all-start.1 = ((f32[4,1,32768]{2,1,0:T(1,128)}), f32[4,1,32768]{2,1,0:T(1,128)S(1)}, u32[]{:S(2)}, u32[]{:S(2)}) async-start(f32[4,1,32768]{2,1,0:T(1,128)} %reshape.99), calls=%async_computation.1 | async-start | bytes 1048576 | tf_op jit(solution)/shard_map/all_to_all | solution.py:64
  38.7 18.5 %all_gather.12 = f32[256,32,8]{1,2,0:T(8,128)S(1)} all-gather(f32[64,32,8]{1,2,0:T(8,128)S(1)} %get-tuple-element.6), channel_id=1, replica_groups=mesh['seq'=4,'res'=8] {'seq'}, dimensions={0}, use_global_device_ids=true | all-gather | bytes 327680 | tf_op jit(solution)/shard_map/all_gather | solution.py:68
  57.2 0.4 copy.49
  57.6 4.3 %all-to-all-start = ((f32[8,8,8,256]{3,2,1,0:T(8,128)}), f32[8,8,8,256]{3,2,1,0:T(8,128)}, u32[]{:S(2)}, u32[]{:S(2)}) async-start(f32[8,8,8,256]{3,2,1,0:T(8,128)} %bitcast), calls=%async_computation | async-start | bytes 1048576 | tf_op jit(solution)/shard_map/all_to_all | solution.py:85
  62.0 0.5 broadcast.97
  62.5 2.1 %reduce.2 = f32[4,32768]{1,0:T(4,128)S(1)} reduce(f32[4,1,32768]{2,1,0:T(1,128)S(1)} %all-to-all-done.1, f32[]{:T(128)} %broadcast.97), dimensions={1}, to_apply=%all_to_all.38.reduce_sub_computation | reduce | bytes 1048580 | tf_op jit(solution)/shard_map/all_to_all | solution.py:64
  64.6 0.5 reshape.100
  65.2 0.7 copy.59
  65.9 0.6 reshape.94
  66.5 3.2 %multiply_bitcast_fusion = f32[16,8,32,32]{2,1,0,3:T(8,128)} fusion(f32[256,32,8,1]{0,2,3,1:T(8,128)S(1)} %copy.49, f32[256,32,16,1]{0,1,2,3:T(8,128)S(1)} %reshape.94), kind=kOutput, calls=%fused_computation.3 | convolution fusion | flops 402784256 | bytes 1310720 | tf_op jit(solution)/shard_map/sxi,syj->ijxy/dot_general | solution.py:65
  69.7 2.3 %copy.42 = f32[16,8,32,32]{3,2,1,0:T(8,128)S(1)} copy(f32[16,8,32,32]{2,1,0,3:T(8,128)} %multiply_bitcast_fusion) | data formatting | bytes 1048576 | tf_op jit(solution)/shard_map/div | solution.py:72
  71.9 0.0 copy-start.6
  72.0 1.7 %div.50 = f32[16,8,1024]{2,1,0:T(8,128)} reshape(f32[16,8,32,32]{3,2,1,0:T(8,128)S(1)} %copy.42) | data formatting | bytes 1048576 | tf_op jit(solution)/shard_map/div | solution.py:72
  73.7 1.9 %fusion.41 = (f32[16,8]{1,0:T(8,128)S(1)}, f32[16,8,128]{2,1,0:T(8,128)S(1)}) fusion(f32[16,8,128]{2,1,0:T(8,128)S(1)} %copy-done.3, f32[16,8,1024]{2,1,0:T(8,128)} %div.50, f32[1024,128]{1,0:T(8,128)} %param.14), kind=kOutput, calls=%fused_computation.60 | convolution fusion | flops 201359232 | bytes 1180160 | tf_op jit(solution)/shard_map/ijk,kc->ijc/dot_general | solution.py:72
  75.6 0.0 copy-start.2
  75.6 0.0 copy-start.4
  75.7 0.2 multiply_reduce_fusion.2
  75.8 0.3 convolution_bitcast_fusion.1
  76.1 14.9 %all_gather.14 = f32[8,16,64]{0,2,1:T(8,128)S(1)} all-gather(f32[8,16,8]{0,2,1:T(8,128)S(1)} %convolution_bitcast_fusion.1), channel_id=1, replica_groups=mesh['seq'=4,'res'=8] {'res'}, dimensions={2}, use_global_device_ids=true | all-gather | bytes 36864 | tf_op jit(solution)/shard_map/all_gather | solution.py:77
  91.1 0.2 copy.43
  91.2 8.4 %all_gather.15 = f32[8,64,64]{2,0,1:T(8,128)S(1)} all-gather(f32[8,16,64]{2,0,1:T(8,128)S(1)} %copy.43), channel_id=1, replica_groups=mesh['seq'=4,'res'=8] {'seq'}, dimensions={1}, use_global_device_ids=true | all-gather | bytes 163840 | tf_op jit(solution)/shard_map/all_gather | solution.py:78
  99.6 0.1 copy.44
  99.8 1.2 bitcast_reduce_fusion
  101.0 0.1 div.42
  101.1 1.3 multiply_reduce_fusion.1
  102.4 0.1 rsqrt.28
  102.5 2.9 %fusion.4 = f32[8,64,1024]{2,1,0:T(8,128)S(1)} fusion(f32[256,1024]{1,0:T(8,128)S(1)} %copy-done, f32[256]{0:T(256)S(1)} %copy-done.4, f32[8,64]{1,0:T(8,128)S(1)} %rsqrt.28, f32[8,64]{1,0:T(8,128)S(1)} %div.42, f32[8,8,8,256]{3,2,1,0:T(8,128)} %all-to-all-done), kind=kOutput, calls=%fused_computation.11 | convolution fusion | flops 1611005952 | bytes 3675136 | tf_op jit(solution)/shard_map/vmap()/dot_general | solution.py:21
  105.5 1.2 fusion.39
  106.7 2.4 %copy.38 = f32[8,64,256]{1,2,0:T(8,128)} copy(f32[8,64,256]{2,1,0:T(8,128)} %get-tuple-element.2) | data formatting | bytes 1048576 | tf_op jit(solution)/shard_map/vmap()/slice | solution.py:27
  109.1 2.4 %copy.37 = f32[8,64,256]{1,2,0:T(8,128)} copy(f32[8,64,256]{2,1,0:T(8,128)} %get-tuple-element.3) | data formatting | bytes 1048576 | tf_op jit(solution)/shard_map/vmap()/mul | solution.py:24
  111.5 2.4 %copy.36 = f32[8,64,256]{1,2,0:T(8,128)} copy(f32[8,64,256]{2,1,0:T(8,128)} %get-tuple-element.4) | data formatting | bytes 1048576 | tf_op jit(solution)/shard_map/vmap()/slice | solution.py:28
  113.8 5.1 %add_reduce_fusion = (f32[8,8,64]{2,1,0:T(8,128)S(1)}, f32[8,8,64,64]{2,3,1,0:T(8,128)S(1)}) fusion(f32[8,64,64]{1,2,0:T(8,128)S(1)} %copy.44, f32[8,64,8,32]{1,3,2,0:T(8,128)} %bitcast.72, f32[8,64,8,32]{1,3,2,0:T(8,128)} %bitcast.71), kind=kOutput, calls=%fused_computation.4 | convolution fusion | flops 101183488 | bytes 2244608 | tf_op jit(solution)/shard_map/vmap(ihd,jhd->hij)/dot_general | solution.py:30
  119.0 0.5 fusion.2
  119.5 0.7 copy-done.1
  120.2 3.3 %fusion = f32[8,8,32,64]{3,2,1,0:T(8,128)} fusion(f32[8,64,8,32]{1,3,2,0:T(8,128)S(1)} %bitcast.78, f32[8,8,64,64]{2,3,1,0:T(8,128)S(1)} %get-tuple-element.10, f32[8,8,64]{2,1,0:T(8,128)S(1)} %fusion.2, f32[8,8,64]{2,1,0:T(8,128)S(1)} %get-tuple-element.9, f32[8,64,64]{1,2,0:T(8,128)S(1)} %copy.44), kind=kOutput, calls=%fused_computation | convolution fusion | flops 101449728 | bytes 2260992 | tf_op jit(solution)/shard_map/vmap(hij,jhd->ihd)/dot_general | solution.py:32
  123.5 2.3 %copy.46 = f32[8,64,256]{2,1,0:T(8,128)} copy(f32[8,64,256]{1,2,0:T(8,128)} %bitcast.79) | data formatting | bytes 1048576 | tf_op jit(solution)/shard_map/vmap()/reshape | solution.py:32
  125.8 1.9 %fusion.3 = f32[1,8,64,256]{3,2,1,0:T(8,128)S(1)} fusion(f32[8,64,256]{2,1,0:T(8,128)} %copy.46, f32[8,64,1024]{2,1,0:T(8,128)S(1)} %fusion.4, f32[256,256]{1,0:T(8,128)} %param.19, f32[8,8,8,256]{3,2,1,0:T(8,128)} %all-to-all-done), kind=kOutput, calls=%fused_computation.7 | convolution fusion | flops 403308544 | bytes 2359296 | tf_op jit(solution)/shard_map/vmap()/dot_general | solution.py:36
  127.8 0.3 copy.47
  128.1 19.8 %all_to_all.48 = f32[1,8,64,256]{3,1,0,2:T(8,128)S(1)} all-to-all(f32[1,8,64,256]{3,1,0,2:T(8,128)S(1)} %copy.47), channel_id=1, replica_groups=mesh['seq'=4,'res'=8] {'res'}, dimensions={2} | all-to-all | bytes 1048576 | tf_op jit(solution)/shard_map/all_to_all | solution.py:92
  148.0 1.0 copy.48
  (19 shorter events, 0.1 us)
Async XLA Ops:
  0.6 101.9 %copy-start = (f32[256,1024]{1,0:T(8,128)S(1)}, f32[256,1024]{1,0:T(8,128)}, u32[]{:S(2)}) copy-start(f32[256,1024]{1,0:T(8,128)} %param.18) | copy-start | bytes 3145732
  35.0 22.6 %all-to-all-start.1 = ((f32[4,1,32768]{2,1,0:T(1,128)}), f32[4,1,32768]{2,1,0:T(1,128)S(1)}, u32[]{:S(2)}, u32[]{:S(2)}) async-start(f32[4,1,32768]{2,1,0:T(1,128)} %reshape.99), calls=%async_computation.1 | async-start | bytes 1048576 | tf_op jit(solution)/shard_map/all_to_all | solution.py:64
  57.6 42.2 %all-to-all-start = ((f32[8,8,8,256]{3,2,1,0:T(8,128)}), f32[8,8,8,256]{3,2,1,0:T(8,128)}, u32[]{:S(2)}, u32[]{:S(2)}) async-start(f32[8,8,8,256]{3,2,1,0:T(8,128)} %bitcast), calls=%async_computation | async-start | bytes 1048576 | tf_op jit(solution)/shard_map/all_to_all | solution.py:85
  71.9 1.8 %copy-start.3 = (f32[16,8,128]{2,1,0:T(8,128)S(1)}, f32[16,8,128]{2,1,0:T(8,128)}, u32[]{:S(2)}) copy-start(f32[16,8,128]{2,1,0:T(8,128)} %param.11) | copy-start | bytes 196612
  71.9 3.9 %copy-start.5 = (f32[128,8]{0,1:T(8,128)S(1)}, f32[128,8]{0,1:T(8,128)}, u32[]{:S(2)}) copy-start(f32[128,8]{0,1:T(8,128)} %param.16) | copy-start | bytes 12292
  71.9 3.9 %copy-start.6 = (f32[128]{0:T(128)S(1)}, f32[128]{0:T(128)}, u32[]{:S(2)}) copy-start(f32[128]{0:T(128)} %param.15) | copy-start | bytes 1540
  75.6 29.8 %copy-start.2 = (f32[16,8,128]{2,1,0:T(8,128)}, f32[16,8,128]{2,1,0:T(8,128)S(1)}, u32[]{:S(2)}) copy-start(f32[16,8,128]{2,1,0:T(8,128)S(1)} %get-tuple-element.8) | copy-start | bytes 196612
  75.6 26.9 %copy-start.4 = (f32[256]{0:T(256)S(1)}, f32[256]{0:T(256)}, u32[]{:S(2)}) copy-start(f32[256]{0:T(256)} %param.17) | copy-start | bytes 3076
  118.9 1.2 copy-start.1
where the time goes:
time: 150 us; the launch traced here: 149 us
  blocking collectives  86.8 us (58%)
  local copies, waits for them, and re-layouts  23.6 us (16%)
  matrix products  20.3 us (14%)
  other arithmetic  9.14 us (6%)
  starting transfers between devices  8.05 us (5%)
    all_gather x1, blocking collectives, on_device(): left_all = lax.all_gather(left_maps, 'res', axis=2, tiled=True)  25.1 us
    all_to_all x1, blocking collectives, on_device(): lax.all_to_all(attended, 'res', split_axis=2, concat_axis=0, tiled=True)  19.8 us
    all_gather x1, blocking collectives, on_device(): lax.all_gather(right_maps, 'seq', axis=0, tiled=True)  18.5 us
    all_gather x1, blocking collectives, on_device(): bias_rows = lax.all_gather(bias_tile, 'res', axis=2, tiled=True)  14.9 us
    all_gather x1, blocking collectives, on_device(): bias_all = lax.all_gather(bias_rows, 'seq', axis=1, tiled=True)  8.4 us
    dot_general x1, matrix products, row_attention(): jnp.einsum('ihd,jhd->hij', query_map, key_map, precision=precise) + bias_all  5.09 us
    all_to_all x1, starting transfers between devices, on_device(): lax.all_to_all(sequence_grouped_rows, 'res', split_axis=0, concat_axis=2,...  4.34 us
    div x2, local copies, waits for them, and re-layouts, on_device(): summed / seq_total  4 us
  transfers between devices with their start and end apart: 2, of which 0 were waited for; matrix products, arithmetic and copies ran while one was open for 10% of the time, Pallas kernels for 0%

commit v1 on v0

--- a/solution.py
+++ b/solution.py
@@ -65,7 +65,9 @@
     product = jnp.einsum(
         "sxi,syj->ijxy",
         left_rows,
-        lax.all_gather(right_maps, "seq", axis=0, tiled=True),
+        jnp.concatenate(
+            lax.all_to_all(jnp.stack([right_maps] * lax.axis_size("seq")), "seq", 0, 0), axis=0
+        ),
         precision=precise,
     )
     summed = product.reshape(row_block, residue_local_count, channels * channels)

time: 150 us -> 147 us (0.980)
  blocking collectives: 86.8 us -> 67.8 us
  starting transfers between devices: 8.05 us -> 13.7 us
  waiting for transfers between devices: 0.01 us -> 5.55 us
  local copies, waits for them, and re-layouts: 23.6 us -> 26.3 us
    all_gather x1 -> x0, blocking collectives: 18.5 us -> none  [on_device(): lax.all_gather(right_maps, 'seq', axis=0, tiled=True)]
    all_to_all x1, waiting for transfers between devices: 0.01 us -> 5.54 us  [on_device(): lax.all_to_all(left_all, 'seq', split_axis=2, concat_axis=0, tiled=True)]
    all_to_all x0 -> x1, starting transfers between devices: none -> 5.19 us  [on_device(): lax.all_to_all(jnp.stack([right_maps] * lax.axis_size('seq')), 'seq', 0, 0)]
    unnamed x16 -> x21, local copies, waits for them, and re-layouts: 3.91 us -> 7.14 us
    dot_general x1, matrix products: 3.15 us -> 4.83 us  [on_device(): jnp.einsum('sxi,syj->ijxy', left_rows, jnp.concatenate(lax.all_to_all(jnp...]
  transfers between devices with their start and end apart: 2 -> 3, of which waited for: 0 -> 1; matrix products, arithmetic and copies ran while one was open for 10% -> 15% of each run, Pallas kernels for 0% -> 0%
where the time goes in v1:
time: 147 us; the launch traced here: 146 us
  blocking collectives  67.8 us (46%)
  local copies, waits for them, and re-layouts  26.3 us (18%)
  matrix products  20.8 us (14%)
  starting transfers between devices  13.7 us (9%)
  other arithmetic  10.5 us (7%)
  waiting for transfers between devices  5.55 us (4%)
    all_gather x1, blocking collectives, on_device(): left_all = lax.all_gather(left_maps, 'res', axis=2, tiled=True)  23.9 us
    all_to_all x1, blocking collectives, on_device(): lax.all_to_all(attended, 'res', split_axis=2, concat_axis=0, tiled=True)  19.8 us
    all_gather x1, blocking collectives, on_device(): bias_rows = lax.all_gather(bias_tile, 'res', axis=2, tiled=True)  14.9 us
    all_gather x1, blocking collectives, on_device(): bias_all = lax.all_gather(bias_rows, 'seq', axis=1, tiled=True)  9.15 us
    unnamed x21, local copies, waits for them, and re-layouts  7.14 us
    all_to_all x1, waiting for transfers between devices, on_device(): lax.all_to_all(left_all, 'seq', split_axis=2, concat_axis=0, tiled=True)  5.54 us
    all_to_all x1, starting transfers between devices, on_device(): lax.all_to_all(jnp.stack([right_maps] * lax.axis_size('seq')), 'seq', 0, 0)  5.19 us
    dot_general x1, matrix products, row_attention(): jnp.einsum('ihd,jhd->hij', query_map, key_map, precision=precise) + bias_all  5.09 us
  transfers between devices with their start and end apart: 3, of which 1 were waited for; matrix products, arithmetic and copies ran while one was open for 15% of the time, Pallas kernels for 0%

profile of v1, /device:TPU:0, one launch (start us, length us, event | category | flops | bytes accessed | tf_op | source)
XLA Modules:
  0.0 145.6 jit_solution(1293706428506713598)
XLA Ops:
  0.6 0.0 copy-start
  0.6 1.3 reduce_sum.65
  1.9 1.3 multiply_reduce_fusion
  3.2 1.7 %convolution_bitcast_fusion = f32[64,64,8]{1,2,0:T(8,128)S(1)} fusion(f32[64,8,256]{2,1,0:T(8,128)} %param.10, f32[256]{0:T(256)} %param.12, f32[64,8]{1,0:T(8,128)S(1)} %add_rsqrt_fusion, f32[64,8]{1,0:T(8,128)S(1)} %broadcast_multiply_fusion, f32[256,64]{0,1:T(8,128)} %param.13), kind=kOutput, calls=%fused_computation.9 | convolution fusion | flops 101056512 | bytes 726016 | tf_op jit(solution)/shard_map/src,cd->sdr/dot_general | solution.py:60
  4.9 0.8 fusion.44
  5.7 0.1 copy.55
  5.8 0.1 broadcast_bitcast_fusion
  5.9 1.0 reshape.104
  7.0 5.2 %all-to-all-start.1 = ((f32[4,1,16384]{2,1,0:T(1,128)}), f32[4,1,16384]{2,1,0:T(1,128)S(1)}, u32[]{:S(2)}, u32[]{:S(2)}) async-start(f32[4,1,16384]{2,1,0:T(1,128)} %reshape.104), calls=%async_computation.1 | async-start | bytes 524288 | tf_op jit(solution)/shard_map/all_to_all | solution.py:69
  12.1 23.9 %all_gather.9 = f32[64,32,64]{1,2,0:T(8,128)S(1)} all-gather(f32[64,32,8]{1,2,0:T(8,128)} %get-tuple-element.6), channel_id=1, replica_groups=mesh['seq'=4,'res'=8] {'res'}, dimensions={2}, use_global_device_ids=true | all-gather | bytes 589824 | tf_op jit(solution)/shard_map/all_gather | solution.py:63
  36.0 2.1 %copy.56 = f32[64,32,64]{0,1,2:T(8,128)} copy(f32[64,32,64]{1,2,0:T(8,128)S(1)} %all_gather.9) | data formatting | bytes 1048576 | tf_op jit(solution)/shard_map/all_gather | solution.py:63
  38.1 2.7 %reshape.102 = f32[4,1,32768]{2,1,0:T(1,128)} reshape(f32[64,32,64]{2,1,0:T(8,128)} %bitcast.86) | data formatting | bytes 1048576
  40.8 4.2 %all-to-all-start.2 = ((f32[4,1,32768]{2,1,0:T(1,128)}), f32[4,1,32768]{2,1,0:T(1,128)S(1)}, u32[]{:S(2)}, u32[]{:S(2)}) async-start(f32[4,1,32768]{2,1,0:T(1,128)} %reshape.102), calls=%async_computation.2 | async-start | bytes 1048576 | tf_op jit(solution)/shard_map/all_to_all | solution.py:64
  45.0 0.5 broadcast.99
  45.5 1.4 reduce.3
  46.9 1.1 reshape.105
  48.0 5.5 %all-to-all-done.2 = f32[4,1,32768]{2,1,0:T(1,128)S(1)} async-done(((f32[4,1,32768]{2,1,0:T(1,128)}), f32[4,1,32768]{2,1,0:T(1,128)S(1)}, u32[]{:S(2)}, u32[]{:S(2)}) %all-to-all-start.2) | async-done | bytes 524320 | tf_op jit(solution)/shard_map/all_to_all | solution.py:64
  53.5 4.3 %all-to-all-start = ((f32[8,8,8,256]{3,2,1,0:T(8,128)}), f32[8,8,8,256]{3,2,1,0:T(8,128)}, u32[]{:S(2)}, u32[]{:S(2)}) async-start(f32[8,8,8,256]{3,2,1,0:T(8,128)} %bitcast), calls=%async_computation | async-start | bytes 1048576 | tf_op jit(solution)/shard_map/all_to_all | solution.py:87
  57.9 2.1 %reduce.2 = f32[4,32768]{1,0:T(4,128)S(1)} reduce(f32[4,1,32768]{2,1,0:T(1,128)S(1)} %all-to-all-done.2, f32[]{:T(128)} %broadcast.99), dimensions={1}, to_apply=%all_to_all.40.reduce_sub_computation | reduce | bytes 1048580 | tf_op jit(solution)/shard_map/all_to_all | solution.py:64
  60.0 1.5 %reshape.103 = f32[64,32,64]{2,1,0:T(8,128)} reshape(f32[4,32768]{1,0:T(4,128)S(1)} %reduce.2) | data formatting | bytes 1048576
  61.5 4.8 %fusion = f32[16,8,32,32]{2,3,0,1:T(8,128)S(1)} fusion(f32[64,32,4,16]{0,1,3,2:T(8,128)} %bitcast.85, f32[4,8,32,64]{3,2,1,0:T(8,128)} %reshape.105), kind=kOutput, calls=%fused_computation.1 | convolution fusion | flops 402784256 | bytes 1310720 | tf_op jit(solution)/shard_map/sxi,syj->ijxy/dot_general | solution.py:65
  66.4 1.9 %copy.60 = f32[16,8,32,32]{3,2,1,0:T(8,128)} copy(f32[16,8,32,32]{2,3,0,1:T(8,128)S(1)} %fusion) | data formatting | bytes 1048576 | tf_op jit(solution)/shard_map/div | solution.py:74
  68.3 2.5 %div.50 = f32[16,8,1024]{2,1,0:T(8,128)S(1)} reshape(f32[16,8,32,32]{3,2,1,0:T(8,128)} %copy.60) | data formatting | bytes 1048576 | tf_op jit(solution)/shard_map/div | solution.py:74
  70.8 0.7 fusion.45
  71.5 0.2 multiply_reduce_fusion.2
  71.7 0.3 convolution_bitcast_fusion.1
  72.0 14.9 %all_gather.10 = f32[8,16,64]{0,2,1:T(8,128)S(1)} all-gather(f32[8,16,8]{0,2,1:T(8,128)S(1)} %convolution_bitcast_fusion.1), channel_id=1, replica_groups=mesh['seq'=4,'res'=8] {'res'}, dimensions={2}, use_global_device_ids=true | all-gather | bytes 36864 | tf_op jit(solution)/shard_map/all_gather | solution.py:79
  87.0 0.2 copy.61
  87.1 9.2 %all_gather.11 = f32[8,64,64]{2,0,1:T(8,128)S(1)} all-gather(f32[8,16,64]{2,0,1:T(8,128)S(1)} %copy.61), channel_id=1, replica_groups=mesh['seq'=4,'res'=8] {'seq'}, dimensions={1}, use_global_device_ids=true | all-gather | bytes 163840 | tf_op jit(solution)/shard_map/all_gather | solution.py:80
  96.3 0.1 copy.62
  96.4 1.2 bitcast_reduce_fusion
  97.7 1.3 multiply_reduce_fusion.1
  99.0 0.1 rsqrt.28
  99.1 0.1 div.42
  99.2 2.9 %fusion.7 = f32[8,64,1024]{2,1,0:T(8,128)S(1)} fusion(f32[256,1024]{1,0:T(8,128)S(1)} %copy-done, f32[256]{0:T(256)S(1)} %copy-done.5, f32[8,64]{1,0:T(8,128)S(1)} %rsqrt.28, f32[8,64]{1,0:T(8,128)S(1)} %div.42, f32[8,8,8,256]{3,2,1,0:T(8,128)} %all-to-all-done), kind=kOutput, calls=%fused_computation.14 | convolution fusion | flops 1611005952 | bytes 3675136 | tf_op jit(solution)/shard_map/vmap()/dot_general | solution.py:21
  102.1 1.2 fusion.43
  103.3 2.4 %copy.53 = f32[8,64,256]{1,2,0:T(8,128)} copy(f32[8,64,256]{2,1,0:T(8,128)} %get-tuple-element.3) | data formatting | bytes 1048576 | tf_op jit(solution)/shard_map/vmap()/mul | solution.py:24
  105.7 2.4 %copy.54 = f32[8,64,256]{1,2,0:T(8,128)} copy(f32[8,64,256]{2,1,0:T(8,128)} %get-tuple-element.2) | data formatting | bytes 1048576 | tf_op jit(solution)/shard_map/vmap()/slice | solution.py:27
  108.1 2.4 %copy.52 = f32[8,64,256]{1,2,0:T(8,128)} copy(f32[8,64,256]{2,1,0:T(8,128)} %get-tuple-element.4) | data formatting | bytes 1048576 | tf_op jit(solution)/shard_map/vmap()/slice | solution.py:28
  110.5 5.1 %add_reduce_fusion = (f32[8,8,64]{2,1,0:T(8,128)S(1)}, f32[8,8,64,64]{2,3,1,0:T(8,128)S(1)}) fusion(f32[8,64,64]{1,2,0:T(8,128)S(1)} %copy.62, f32[8,64,8,32]{1,3,2,0:T(8,128)} %bitcast.83, f32[8,64,8,32]{1,3,2,0:T(8,128)} %bitcast.84), kind=kOutput, calls=%fused_computation.5 | convolution fusion | flops 101183488 | bytes 2244608 | tf_op jit(solution)/shard_map/vmap(ihd,jhd->hij)/dot_general | solution.py:30
  115.6 0.5 fusion.3
  116.2 0.7 copy-done.1
  116.8 3.3 %fusion.1 = f32[8,8,32,64]{3,2,1,0:T(8,128)} fusion(f32[8,64,8,32]{1,3,2,0:T(8,128)S(1)} %bitcast.88, f32[8,8,64,64]{2,3,1,0:T(8,128)S(1)} %get-tuple-element.10, f32[8,8,64]{2,1,0:T(8,128)S(1)} %fusion.3, f32[8,8,64]{2,1,0:T(8,128)S(1)} %get-tuple-element.9, f32[8,64,64]{1,2,0:T(8,128)S(1)} %copy.62), kind=kOutput, calls=%fused_computation.2 | convolution fusion | flops 101449728 | bytes 2260992 | tf_op jit(solution)/shard_map/vmap(hij,jhd->ihd)/dot_general | solution.py:32
  120.2 2.3 %copy.64 = f32[8,64,256]{2,1,0:T(8,128)} copy(f32[8,64,256]{1,2,0:T(8,128)} %bitcast.89) | data formatting | bytes 1048576 | tf_op jit(solution)/shard_map/vmap()/reshape | solution.py:32
  122.5 2.0 %fusion.4 = f32[1,8,64,256]{3,2,1,0:T(8,128)S(1)} fusion(f32[8,64,256]{2,1,0:T(8,128)} %copy.64, f32[8,64,1024]{2,1,0:T(8,128)S(1)} %fusion.7, f32[256,256]{1,0:T(8,128)} %param.19, f32[8,8,8,256]{3,2,1,0:T(8,128)} %all-to-all-done), kind=kOutput, calls=%fused_computation.8 | convolution fusion | flops 403308544 | bytes 2359296 | tf_op jit(solution)/shard_map/vmap()/dot_general | solution.py:36
  124.5 0.3 copy.65
  124.8 19.8 %all_to_all.50 = f32[1,8,64,256]{3,1,0,2:T(8,128)S(1)} all-to-all(f32[1,8,64,256]{3,1,0,2:T(8,128)S(1)} %copy.65), channel_id=1, replica_groups=mesh['seq'=4,'res'=8] {'res'}, dimensions={2} | all-to-all | bytes 1048576 | tf_op jit(solution)/shard_map/all_to_all | solution.py:94
  144.6 1.0 copy.66
  (24 shorter events, 0.1 us)
Async XLA Ops:
  0.6 98.5 %copy-start = (f32[256,1024]{1,0:T(8,128)S(1)}, f32[256,1024]{1,0:T(8,128)}, u32[]{:S(2)}) copy-start(f32[256,1024]{1,0:T(8,128)} %param.18) | copy-start | bytes 3145732
  7.0 33.9 %all-to-all-start.1 = ((f32[4,1,16384]{2,1,0:T(1,128)}), f32[4,1,16384]{2,1,0:T(1,128)S(1)}, u32[]{:S(2)}, u32[]{:S(2)}) async-start(f32[4,1,16384]{2,1,0:T(1,128)} %reshape.104), calls=%async_computation.1 | async-start | bytes 524288 | tf_op jit(solution)/shard_map/all_to_all | solution.py:69
  40.8 12.7 %all-to-all-start.2 = ((f32[4,1,32768]{2,1,0:T(1,128)}), f32[4,1,32768]{2,1,0:T(1,128)S(1)}, u32[]{:S(2)}, u32[]{:S(2)}) async-start(f32[4,1,32768]{2,1,0:T(1,128)} %reshape.102), calls=%async_computation.2 | async-start | bytes 1048576 | tf_op jit(solution)/shard_map/all_to_all | solution.py:64
  53.5 42.9 %all-to-all-start = ((f32[8,8,8,256]{3,2,1,0:T(8,128)}), f32[8,8,8,256]{3,2,1,0:T(8,128)}, u32[]{:S(2)}, u32[]{:S(2)}) async-start(f32[8,8,8,256]{3,2,1,0:T(8,128)} %bitcast), calls=%async_computation | async-start | bytes 1048576 | tf_op jit(solution)/shard_map/all_to_all | solution.py:87
  68.2 2.5 %copy-start.2 = (f32[1024,128]{1,0:T(8,128)S(1)}, f32[1024,128]{1,0:T(8,128)}, u32[]{:S(2)}) copy-start(f32[1024,128]{1,0:T(8,128)} %param.14) | copy-start | bytes 1572868
  68.3 2.5 %copy-start.4 = (f32[16,8,128]{2,1,0:T(8,128)S(1)}, f32[16,8,128]{2,1,0:T(8,128)}, u32[]{:S(2)}) copy-start(f32[16,8,128]{2,1,0:T(8,128)} %param.11) | copy-start | bytes 196612
  68.3 3.5 %copy-start.6 = (f32[128,8]{0,1:T(8,128)S(1)}, f32[128,8]{0,1:T(8,128)}, u32[]{:S(2)}) copy-start(f32[128,8]{0,1:T(8,128)} %param.16) | copy-start | bytes 12292
  68.3 3.5 %copy-start.7 = (f32[128]{0:T(128)S(1)}, f32[128]{0:T(128)}, u32[]{:S(2)}) copy-start(f32[128]{0:T(128)} %param.15) | copy-start | bytes 1540
  71.5 30.6 %copy-start.3 = (f32[16,8,128]{2,1,0:T(8,128)}, f32[16,8,128]{2,1,0:T(8,128)S(1)}, u32[]{:S(2)}) copy-start(f32[16,8,128]{2,1,0:T(8,128)S(1)} %get-tuple-element.8) | copy-start | bytes 196612
  71.5 27.7 %copy-start.5 = (f32[256]{0:T(256)S(1)}, f32[256]{0:T(256)}, u32[]{:S(2)}) copy-start(f32[256]{0:T(256)} %param.17) | copy-start | bytes 3076
  115.6 1.2 copy-start.1
